TPU v7x, 32 devices: a whole 2x2x4 slice. The times are simulated.
32 devices in a mesh: wide: 8 (over z, x), narrow: 4 (over y, core).
Axes of the slice: x: 2, y: 2, z: 4, core: 2. Of those that a mesh axis runs over, the one named last changes fastest.
Arguments:
- embeddings: bfloat16 [8192, 512], P(('wide', 'narrow')), may hold values from -26 to 26
- partners: int32 [32, 7], P(('wide', 'narrow')), may hold values from -1 to 7, as said below
- pair_kind: int32 [32, 7], P(('wide', 'narrow')), may hold values from 0 to 1, as said below
- neighbors: int32 [7, 15, 8192], P(None, None, ('wide', 'narrow')), may hold values from 0 to 255
Outputs:
- gradient: float32 [8192, 512], P(('wide', 'narrow'))
- mean_loss: float32 [], replicated
Inputs may be any that keep to these rules, and one draw needn't show every extreme that they name: Row w * 4 + n lists the wide indices of that block's partners in ascending order, then -1 in the remaining slots; a partner has the same narrow index n, is never the block itself, appears once, and the pairing is mutual. In every narrow index one block is paired with all 7 others. `pair_kind`: 1 marks a graph pair, 0 a sampled negative or an empty slot; both directions of a pair carry the same mark, and every block has at least one graph pair.
All inputs are finite; a program needn't handle non-finite values.
Results may differ from a plain program's by a relative error of at most 0.0004.
Values may be sent and summed in bfloat16 or wider, within the bound.
No kernel may reach another device: no remote copies, remote signals or barrier semaphores. Data moves between devices by JAX's collectives and lax.ppermute only.
A program may use at most 64 MiB of HBM per device.

v0:
```python
import jax
import jax.numpy as jnp
from jax import lax
from jax.sharding import PartitionSpec as P


def tile_kernel(local_rows, remote_rows, local_norms, features):
    remote_norms = jnp.sum(jnp.square(remote_rows.astype(jnp.float32)), axis=1)
    inner = jnp.einsum("id,jd->ij", local_rows, remote_rows, preferred_element_type=jnp.float32)
    distance = local_norms[:, None] + remote_norms[None, :] - 2.0 * inner
    return 1.0 / (1.0 + distance / features)


def edge_counts(targets, block_rows):
    columns = lax.broadcasted_iota(jnp.int32, (1, 1, block_rows), 2)
    return jnp.sum((targets[:, :, None] == columns).astype(jnp.float32), axis=0)


def mirrored_counts(sources, block_rows):
    rows_index = lax.broadcasted_iota(jnp.int32, (1, block_rows, 1), 1)
    return jnp.sum((sources[:, None, :] == rows_index).astype(jnp.float32), axis=0)


def per_device(embeddings, partners, pair_kind, neighbors):
    block_rows, features = embeddings.shape
    slot_count = partners.shape[1]
    groups = lax.axis_size("wide")
    column = lax.all_gather(embeddings, "wide", axis=0, tiled=True).reshape(
        groups, block_rows, features
    )
    local_float = embeddings.astype(jnp.float32)
    local_norms = jnp.sum(jnp.square(local_float), axis=1)
    partner_row = partners[0]
    mark_row = pair_kind[0].astype(jnp.float32)

    def remote_of(slot):
        partner = partner_row[slot]
        return (
            partner,
            lax.dynamic_index_in_dim(column, jnp.maximum(partner, 0), 0, keepdims=False),
        )

    def first(slot, carry):

        def first_active(carry):
            sums, kernels, counts_store = carry
            partner, remote_rows = remote_of(slot)
            kernel = tile_kernel(embeddings, remote_rows, local_norms, features)
            targets = lax.dynamic_index_in_dim(neighbors, slot, 0, keepdims=False)
            counts = edge_counts(targets, block_rows) * mark_row[slot]
            sums = (
                sums[0] + jnp.sum(kernel),
                sums[1] + jnp.sum(counts * jnp.log(kernel)),
                sums[2] + jnp.sum(counts),
                sums[3] + float(block_rows * block_rows),
            )
            kernels = lax.dynamic_update_index_in_dim(kernels, kernel, slot, 0)
            counts_store = lax.dynamic_update_index_in_dim(counts_store, counts, slot, 0)
            return (sums, kernels, counts_store)

        return lax.cond(partner_row[slot] >= 0, first_active, lambda carry: carry, carry)

    nothing = jnp.zeros((), jnp.float32)
    empty_tiles = jnp.zeros((slot_count, block_rows, block_rows), jnp.float32)
    sums, kernels, counts_store = lax.fori_loop(
        0, slot_count, first, ((nothing, nothing, nothing, nothing), empty_tiles, empty_tiles)
    )
    kernel_sum, attract_sum, edge_sum, entry_sum = sums
    total, attract, edges_total, entries = lax.psum(
        (kernel_sum, attract_sum, edge_sum, entry_sum), ("wide", "narrow")
    )
    mean_loss = -attract / edges_total + jnp.log(total / entries)
    repulsion = edges_total / total
    start_gradient = jnp.zeros((block_rows, features), jnp.float32)
    selector = (partner_row[None, :] == lax.broadcasted_iota(jnp.int32, (groups, 1), 0)).astype(
        jnp.int32
    )
    outgoing = jnp.tensordot(selector, neighbors, axes=1)
    incoming = lax.all_to_all(outgoing, "wide", split_axis=0, concat_axis=0, tiled=True)

    def second(slot, gradient):

        def second_active(gradient):
            partner, remote_rows = remote_of(slot)
            kernel = lax.dynamic_index_in_dim(kernels, slot, 0, keepdims=False)
            counts = lax.dynamic_index_in_dim(counts_store, slot, 0, keepdims=False)
            sources = lax.dynamic_index_in_dim(incoming, jnp.maximum(partner, 0), 0, keepdims=False)
            back_counts = mirrored_counts(sources, block_rows) * mark_row[slot]
            weight = (counts * kernel - repulsion * kernel * kernel) / features
            mirror = (back_counts * kernel - repulsion * kernel * kernel) / features
            row_total = jnp.sum(weight, axis=1) + jnp.sum(mirror, axis=1)
            product = jnp.dot(
                weight.astype(jnp.bfloat16), remote_rows, preferred_element_type=jnp.float32
            ) + jnp.dot(
                mirror.astype(jnp.bfloat16), remote_rows, preferred_element_type=jnp.float32
            )
            return gradient + 2.0 * (row_total[:, None] * local_float - product)

        return lax.cond(partner_row[slot] >= 0, second_active, lambda gradient: gradient, gradient)

    gradient = lax.fori_loop(0, slot_count, second, start_gradient)
    return (gradient, mean_loss)


def solution(mesh):
    in_specs = (
        P(("wide", "narrow"), None),
        P(("wide", "narrow"), None),
        P(("wide", "narrow"), None),
        P(None, None, ("wide", "narrow")),
    )
    out_specs = (P(("wide", "narrow"), None), P())
    return jax.shard_map(
        per_device, mesh=mesh, in_specs=in_specs, out_specs=out_specs, check_vma=False
    )
```

profile of v0, /device:TPU:0, one launch (start us, length us, event | category | flops | bytes accessed | tf_op | source)
XLA Modules:
  0.0 261.6 jit_solution(13438871651944459247)
XLA Ops:
  9.8 7.3 %all-to-all-start = ((s32[8,15,256]{2,1,0:T(8,128)}), s32[8,15,256]{2,1,0:T(8,128)S(1)}, u32[]{:S(2)}, u32[]{:S(2)}) async-start(s32[8,15,256]{2,1,0:T(8,128)} %copy.16), calls=%async_computation | async-start | bytes 262144 | tf_op jit(solution)/shard_map/all_to_all | solution.py:79
  18.2 43.7 %all-gather.2.cloned.1.call-done = bf16[2048,512]{1,0:T(8,128)(2,1)} async-done(((bf16[256,512]{1,0:T(8,128)(2,1)}), bf16[2048,512]{1,0:T(8,128)(2,1)}) %all-gather.2.cloned.1.call-update) | async-done | bytes 2097168 | tf_op jit(solution)/shard_map/all_gather | solution.py:28
  63.5 80.1 %while.39 = (s32[]{:T(128)}, f32[]{:T(128)}, f32[]{:T(128)}, f32[]{:T(128)}, f32[]{:T(128)}, /*index=5*/f32[7,256,256]{1,2,0:T(8,128)S(1)}, f32[7,256,256]{1,2,0...) while((s32[]{:T(128)}, f32[]{:T(128)}, f32[]{:T(128)}, ...), condition=%wide.region_9.10_spmd, body=%wide.region_1.9_spmd.sunk | while | flops 71171840 | bytes 3196933 | solution.py:65
  64.8 10.2 %conditional.4 = ((f32[]{:T(128)}, f32[]{:T(128)}, f32[]{:T(128)}, f32[]{:T(128)}, f32[7,256,256]{1,2,0:T(8,128)S(1)}, /*index=5*/f32[7,256,256]{1,2,0:T(8,128)})) conditional(s32[]{:T(128)} %bitcast.84, (f32[]{:T(128)}, f32[]{:T(128)}, f32[]{:T(128)}, f32[]{:T(128)}, f32[7,256,256]{1,2,0:T(8,128)S(1)}, ...), branch_computations={%region_2.0_spmd, %region_3.8_spmd} | conditional | flops 71171840 | bytes 3196614 | solution.py:61
  69.3 2.6 multiply_reduce_fusion.2
  76.2 10.2 %conditional.4 = ((f32[]{:T(128)}, f32[]{:T(128)}, f32[]{:T(128)}, f32[]{:T(128)}, f32[7,256,256]{1,2,0:T(8,128)S(1)}, /*index=5*/f32[7,256,256]{1,2,0:T(8,128)})) conditional(s32[]{:T(128)} %bitcast.84, (f32[]{:T(128)}, f32[]{:T(128)}, f32[]{:T(128)}, f32[]{:T(128)}, f32[7,256,256]{1,2,0:T(8,128)S(1)}, ...), branch_computations={%region_2.0_spmd, %region_3.8_spmd} | conditional | flops 71171840 | bytes 3196614 | solution.py:61
  80.7 2.5 multiply_reduce_fusion.2
  87.6 10.2 %conditional.4 = ((f32[]{:T(128)}, f32[]{:T(128)}, f32[]{:T(128)}, f32[]{:T(128)}, f32[7,256,256]{1,2,0:T(8,128)S(1)}, /*index=5*/f32[7,256,256]{1,2,0:T(8,128)})) conditional(s32[]{:T(128)} %bitcast.84, (f32[]{:T(128)}, f32[]{:T(128)}, f32[]{:T(128)}, f32[]{:T(128)}, f32[7,256,256]{1,2,0:T(8,128)S(1)}, ...), branch_computations={%region_2.0_spmd, %region_3.8_spmd} | conditional | flops 71171840 | bytes 3196614 | solution.py:61
  92.1 2.5 multiply_reduce_fusion.2
  99.1 10.2 %conditional.4 = ((f32[]{:T(128)}, f32[]{:T(128)}, f32[]{:T(128)}, f32[]{:T(128)}, f32[7,256,256]{1,2,0:T(8,128)S(1)}, /*index=5*/f32[7,256,256]{1,2,0:T(8,128)})) conditional(s32[]{:T(128)} %bitcast.84, (f32[]{:T(128)}, f32[]{:T(128)}, f32[]{:T(128)}, f32[]{:T(128)}, f32[7,256,256]{1,2,0:T(8,128)S(1)}, ...), branch_computations={%region_2.0_spmd, %region_3.8_spmd} | conditional | flops 71171840 | bytes 3196614 | solution.py:61
  103.6 2.5 multiply_reduce_fusion.2
  110.5 10.2 %conditional.4 = ((f32[]{:T(128)}, f32[]{:T(128)}, f32[]{:T(128)}, f32[]{:T(128)}, f32[7,256,256]{1,2,0:T(8,128)S(1)}, /*index=5*/f32[7,256,256]{1,2,0:T(8,128)})) conditional(s32[]{:T(128)} %bitcast.84, (f32[]{:T(128)}, f32[]{:T(128)}, f32[]{:T(128)}, f32[]{:T(128)}, f32[7,256,256]{1,2,0:T(8,128)S(1)}, ...), branch_computations={%region_2.0_spmd, %region_3.8_spmd} | conditional | flops 71171840 | bytes 3196614 | solution.py:61
  115.0 2.5 multiply_reduce_fusion.2
  122.0 10.2 %conditional.4 = ((f32[]{:T(128)}, f32[]{:T(128)}, f32[]{:T(128)}, f32[]{:T(128)}, f32[7,256,256]{1,2,0:T(8,128)S(1)}, /*index=5*/f32[7,256,256]{1,2,0:T(8,128)})) conditional(s32[]{:T(128)} %bitcast.84, (f32[]{:T(128)}, f32[]{:T(128)}, f32[]{:T(128)}, f32[]{:T(128)}, f32[7,256,256]{1,2,0:T(8,128)S(1)}, ...), branch_computations={%region_2.0_spmd, %region_3.8_spmd} | conditional | flops 71171840 | bytes 3196614 | solution.py:61
  126.5 2.6 multiply_reduce_fusion.2
  133.4 10.2 %conditional.4 = ((f32[]{:T(128)}, f32[]{:T(128)}, f32[]{:T(128)}, f32[]{:T(128)}, f32[7,256,256]{1,2,0:T(8,128)S(1)}, /*index=5*/f32[7,256,256]{1,2,0:T(8,128)})) conditional(s32[]{:T(128)} %bitcast.84, (f32[]{:T(128)}, f32[]{:T(128)}, f32[]{:T(128)}, f32[]{:T(128)}, f32[7,256,256]{1,2,0:T(8,128)S(1)}, ...), branch_computations={%region_2.0_spmd, %region_3.8_spmd} | conditional | flops 71171840 | bytes 3196614 | solution.py:61
  137.9 2.5 multiply_reduce_fusion.2
  143.6 41.4 %all-reduce = (f32[]{:T(128)}, f32[]{:T(128)}, f32[]{:T(128)}, f32[]{:T(128)}) all-reduce(f32[]{:T(128)} %get-tuple-element.499, f32[]{:T(128)} %get-tuple-element.500, f32[]{:T(128)} %get-tuple-element.502, f32[]{:T(128)} %get-tuple-element.503), channel_id=1, replica_groups=mesh['wide'=8,'narrow'=4] {'wide','narrow'}, use_global_device_ids=true, to_apply=%region_10.11 | all-reduce | flops 4 | bytes 32 | tf_op jit(solution)/shard_map/psum | solution.py:69
  189.0 2.7 %copy.17 = f32[7,256,256]{2,1,0:T(8,128)} copy(f32[7,256,256]{1,2,0:T(8,128)} %get-tuple-element.527) | data formatting | bytes 3670016 | tf_op jit(solution)/shard_map/while | solution.py:101
  193.6 59.2 %while.40 = (s32[]{:T(128)}, f32[256,512]{1,0:T(8,128)S(1)}, s32[7]{0:T(128)S(1)}, f32[7,256,256]{2,1,0:T(8,128)}, f32[7,256,256]{2,1,0:T(8,128)S(1)}, /*index=5...) while((s32[]{:T(128)}, f32[256,512]{1,0:T(8,128)S(1)}, ...), condition=%wide.region_18.19_spmd, body=%wide.region_12.18_spmd.sunk | while | flops 139329280 | bytes 5297989 | solution.py:101
  194.9 7.2 %conditional.5 = (f32[256,512]{1,0:T(8,128)S(1)}) conditional(s32[]{:T(128)} %bitcast.85, f32[256,512]{1,0:T(8,128)S(1)} %get-tuple-element.814, (s32[]{:T(128)}, f32[7,256,256]{2,1,0:T(8,128)}, f32[7,256,256]{2,1,0:T(8,128)S(1)}, f32[]{:T(128)}, s32[7]{0:T(128)S(1)}, /*index=5*/s32[8,15,256]{2,1,0:T(8,128)S(1)}, f32[7]{0:T(128)S(1)}, ...), branch_computations={%region_13.13_spmd, %region_14.17_spmd} | conditional | flops 139329280 | bytes 5297766 | solution.py:99
  200.3 1.8 fusion.10
  203.3 7.2 %conditional.5 = (f32[256,512]{1,0:T(8,128)S(1)}) conditional(s32[]{:T(128)} %bitcast.85, f32[256,512]{1,0:T(8,128)S(1)} %get-tuple-element.814, (s32[]{:T(128)}, f32[7,256,256]{2,1,0:T(8,128)}, f32[7,256,256]{2,1,0:T(8,128)S(1)}, f32[]{:T(128)}, s32[7]{0:T(128)S(1)}, /*index=5*/s32[8,15,256]{2,1,0:T(8,128)S(1)}, f32[7]{0:T(128)S(1)}, ...), branch_computations={%region_13.13_spmd, %region_14.17_spmd} | conditional | flops 139329280 | bytes 5297766 | solution.py:99
  208.7 1.8 fusion.10
  211.8 7.2 %conditional.5 = (f32[256,512]{1,0:T(8,128)S(1)}) conditional(s32[]{:T(128)} %bitcast.85, f32[256,512]{1,0:T(8,128)S(1)} %get-tuple-element.814, (s32[]{:T(128)}, f32[7,256,256]{2,1,0:T(8,128)}, f32[7,256,256]{2,1,0:T(8,128)S(1)}, f32[]{:T(128)}, s32[7]{0:T(128)S(1)}, /*index=5*/s32[8,15,256]{2,1,0:T(8,128)S(1)}, f32[7]{0:T(128)S(1)}, ...), branch_computations={%region_13.13_spmd, %region_14.17_spmd} | conditional | flops 139329280 | bytes 5297766 | solution.py:99
  217.2 1.8 fusion.10
  220.3 7.2 %conditional.5 = (f32[256,512]{1,0:T(8,128)S(1)}) conditional(s32[]{:T(128)} %bitcast.85, f32[256,512]{1,0:T(8,128)S(1)} %get-tuple-element.814, (s32[]{:T(128)}, f32[7,256,256]{2,1,0:T(8,128)}, f32[7,256,256]{2,1,0:T(8,128)S(1)}, f32[]{:T(128)}, s32[7]{0:T(128)S(1)}, /*index=5*/s32[8,15,256]{2,1,0:T(8,128)S(1)}, f32[7]{0:T(128)S(1)}, ...), branch_computations={%region_13.13_spmd, %region_14.17_spmd} | conditional | flops 139329280 | bytes 5297766 | solution.py:99
  228.7 7.2 %conditional.5 = (f32[256,512]{1,0:T(8,128)S(1)}) conditional(s32[]{:T(128)} %bitcast.85, f32[256,512]{1,0:T(8,128)S(1)} %get-tuple-element.814, (s32[]{:T(128)}, f32[7,256,256]{2,1,0:T(8,128)}, f32[7,256,256]{2,1,0:T(8,128)S(1)}, f32[]{:T(128)}, s32[7]{0:T(128)S(1)}, /*index=5*/s32[8,15,256]{2,1,0:T(8,128)S(1)}, f32[7]{0:T(128)S(1)}, ...), branch_computations={%region_13.13_spmd, %region_14.17_spmd} | conditional | flops 139329280 | bytes 5297766 | solution.py:99
  234.1 1.8 fusion.10
  237.2 7.2 %conditional.5 = (f32[256,512]{1,0:T(8,128)S(1)}) conditional(s32[]{:T(128)} %bitcast.85, f32[256,512]{1,0:T(8,128)S(1)} %get-tuple-element.814, (s32[]{:T(128)}, f32[7,256,256]{2,1,0:T(8,128)}, f32[7,256,256]{2,1,0:T(8,128)S(1)}, f32[]{:T(128)}, s32[7]{0:T(128)S(1)}, /*index=5*/s32[8,15,256]{2,1,0:T(8,128)S(1)}, f32[7]{0:T(128)S(1)}, ...), branch_computations={%region_13.13_spmd, %region_14.17_spmd} | conditional | flops 139329280 | bytes 5297766 | solution.py:99
  245.6 7.2 %conditional.5 = (f32[256,512]{1,0:T(8,128)S(1)}) conditional(s32[]{:T(128)} %bitcast.85, f32[256,512]{1,0:T(8,128)S(1)} %get-tuple-element.814, (s32[]{:T(128)}, f32[7,256,256]{2,1,0:T(8,128)}, f32[7,256,256]{2,1,0:T(8,128)S(1)}, f32[]{:T(128)}, s32[7]{0:T(128)S(1)}, /*index=5*/s32[8,15,256]{2,1,0:T(8,128)S(1)}, f32[7]{0:T(128)S(1)}, ...), branch_computations={%region_13.13_spmd, %region_14.17_spmd} | conditional | flops 139329280 | bytes 5297766 | solution.py:99
  251.0 1.8 fusion.10
  (136 shorter events, 89.6 us)
Async XLA Ops:
  7.2 10.9 %copy-start.2 = (bf16[256,512]{1,0:T(8,128)(2,1)S(1)}, bf16[256,512]{1,0:T(8,128)(2,1)}, u32[]{:S(2)}) copy-start(bf16[256,512]{1,0:T(8,128)(2,1)} %param.12) | copy-start | bytes 786436
  7.2 11.0 %copy-start.4 = (s32[1,7]{1,0:T(1,128)S(1)}, s32[1,7]{1,0:T(1,128)}, u32[]{:S(2)}) copy-start(s32[1,7]{1,0:T(1,128)} %param.14) | copy-start | bytes 88
  7.2 54.8 %all-gather.2.cloned.1.call-start = ((), (), s32[]{:S(2)}) async-start(), calls=%async_computation.1 | async-start | bytes 2359296 | tf_op jit(solution)/shard_map/all_gather | solution.py:28
  9.8 183.8 %all-to-all-start = ((s32[8,15,256]{2,1,0:T(8,128)}), s32[8,15,256]{2,1,0:T(8,128)S(1)}, u32[]{:S(2)}, u32[]{:S(2)}) async-start(s32[8,15,256]{2,1,0:T(8,128)} %copy.16), calls=%async_computation | async-start | bytes 262144 | tf_op jit(solution)/shard_map/all_to_all | solution.py:79
  62.0 1.6 copy-start.3
  143.6 48.1 %copy-start.1 = (f32[7,256,256]{1,2,0:T(8,128)}, f32[7,256,256]{1,2,0:T(8,128)S(1)}, u32[]{:S(2)}) copy-start(f32[7,256,256]{1,2,0:T(8,128)S(1)} %get-tuple-element.528) | copy-start | bytes 5505028
  252.9 0.8 copy-start
Sparse Core Ops, SparseCore 0:
  10.1 51.8 all-gather.1
where the time goes:
time: 264 us; the launch traced here: 262 us
  waiting for transfers between devices  44.4 us (17%)
  blocking collectives  41.4 us (16%)
  matrix products  40.6 us (15%)
  other arithmetic  39.2 us (15%)
  local copies, waits for them, and re-layouts  38.7 us (15%)
  loops' own time  30.7 us (12%)
  between operations  19.2 us (7%)
  starting transfers between devices  7.32 us (3%)
    all_gather x1, waiting for transfers between devices, per_device(): lax.all_gather(embeddings, 'wide', axis=0, tiled=True)  43.7 us
    psum x1, blocking collectives, per_device(): lax.psum((kernel_sum, attract_sum, edge_sum, entry_sum), ('wide', 'narrow'))  41.4 us
    dot_general x7, matrix products, tile_kernel(): jnp.einsum('id,jd->ij', local_rows, remote_rows, preferred_element_type=j...  17.8 us
    another operation x7, loops' own time, first(): lax.cond(partner_row[slot] >= 0, first_active, lambda carry: carry, carry)  16.8 us
    dot_general x7, matrix products, second_active(): jnp.dot(mirror.astype(jnp.bfloat16), remote_rows, preferred_element_type=...  12.8 us
    reduce_sum x7, other arithmetic, second_active(): row_total = jnp.sum(weight, axis=1) + jnp.sum(mirror, axis=1)  12.2 us
    dynamic_update_slice x7, other arithmetic, first_active(): lax.dynamic_update_index_in_dim(counts_store, counts, slot, 0)  9.57 us
    dot_general x7, matrix products, second_active(): jnp.dot(weight.astype(jnp.bfloat16), remote_rows, preferred_element_type=...  8.86 us
  transfers between devices with their start and end apart: 2, of which 1 were waited for; matrix products, arithmetic and copies ran while one was open for 26% of the time, Pallas kernels for 0%

commit v1 on v0

--- a/solution.py
+++ b/solution.py
@@ -2,6 +2,12 @@
 import jax.numpy as jnp
 from jax import lax
 from jax.sharding import PartitionSpec as P
+
+
+def mark_cubes(target, lane_axis, link_axis):
+    for it in (lane_axis, link_axis):
+        target = lax.psum(target, it)
+    return target
 
 
 def tile_kernel(local_rows, remote_rows, local_norms, features):
@@ -66,8 +72,8 @@
         0, slot_count, first, ((nothing, nothing, nothing, nothing), empty_tiles, empty_tiles)
     )
     kernel_sum, attract_sum, edge_sum, entry_sum = sums
-    total, attract, edges_total, entries = lax.psum(
-        (kernel_sum, attract_sum, edge_sum, entry_sum), ("wide", "narrow")
+    total, attract, edges_total, entries = mark_cubes(
+        (kernel_sum, attract_sum, edge_sum, entry_sum), lane_axis="wide", link_axis="narrow"
     )
     mean_loss = -attract / edges_total + jnp.log(total / entries)
     repulsion = edges_total / total

time: 264 us -> 249 us (0.943)
  blocking collectives: 41.4 us -> 26.4 us
    psum x1 -> x2, blocking collectives: 41.4 us -> 26.4 us  [mark_cubes(): target = lax.psum(target, it)]
  transfers between devices with their start and end apart: 2 -> 2, of which waited for: 1 -> 1; matrix products, arithmetic and copies ran while one was open for 26% -> 28% of each run, Pallas kernels for 0% -> 0%
where the time goes in v1:
time: 249 us; the launch traced here: 247 us
  waiting for transfers between devices  44.4 us (18%)
  matrix products  40.6 us (16%)
  other arithmetic  39.2 us (16%)
  local copies, waits for them, and re-layouts  38.7 us (16%)
  loops' own time  30.7 us (12%)
  blocking collectives  26.4 us (11%)
  between operations  19.1 us (8%)
  starting transfers between devices  7.32 us (3%)
    all_gather x1, waiting for transfers between devices, per_device(): lax.all_gather(embeddings, 'wide', axis=0, tiled=True)  43.7 us
    psum x2, blocking collectives, mark_cubes(): target = lax.psum(target, it)  26.4 us
    dot_general x7, matrix products, tile_kernel(): jnp.einsum('id,jd->ij', local_rows, remote_rows, preferred_element_type=j...  17.8 us
    another operation x7, loops' own time, first(): lax.cond(partner_row[slot] >= 0, first_active, lambda carry: carry, carry)  16.8 us
    dot_general x7, matrix products, second_active(): jnp.dot(mirror.astype(jnp.bfloat16), remote_rows, preferred_element_type=...  12.8 us
    reduce_sum x7, other arithmetic, second_active(): row_total = jnp.sum(weight, axis=1) + jnp.sum(mirror, axis=1)  12.2 us
    dynamic_update_slice x7, other arithmetic, first_active(): lax.dynamic_update_index_in_dim(counts_store, counts, slot, 0)  9.57 us
    dot_general x7, matrix products, second_active(): jnp.dot(weight.astype(jnp.bfloat16), remote_rows, preferred_element_type=...  8.86 us
  transfers between devices with their start and end apart: 2, of which 1 were waited for; matrix products, arithmetic and copies ran while one was open for 28% of the time, Pallas kernels for 0%

profile of v1, /device:TPU:0, one launch (start us, length us, event | category | flops | bytes accessed | tf_op | source)
XLA Modules:
  0.0 246.5 jit_solution(6365610034684461545)
XLA Ops:
  9.8 7.3 %all-to-all-start = ((s32[8,15,256]{2,1,0:T(8,128)}), s32[8,15,256]{2,1,0:T(8,128)S(1)}, u32[]{:S(2)}, u32[]{:S(2)}) async-start(s32[8,15,256]{2,1,0:T(8,128)} %copy.16), calls=%async_computation | async-start | bytes 262144 | tf_op jit(solution)/shard_map/all_to_all | solution.py:85
  18.2 43.7 %all-gather.2.cloned.1.call-done = bf16[2048,512]{1,0:T(8,128)(2,1)} async-done(((bf16[256,512]{1,0:T(8,128)(2,1)}), bf16[2048,512]{1,0:T(8,128)(2,1)}) %all-gather.2.cloned.1.call-update) | async-done | bytes 2097168 | tf_op jit(solution)/shard_map/all_gather | solution.py:34
  63.5 80.1 %while.39 = (s32[]{:T(128)}, f32[]{:T(128)}, f32[]{:T(128)}, f32[]{:T(128)}, f32[]{:T(128)}, /*index=5*/f32[7,256,256]{1,2,0:T(8,128)S(1)}, f32[7,256,256]{1,2,0...) while((s32[]{:T(128)}, f32[]{:T(128)}, f32[]{:T(128)}, ...), condition=%wide.region_9.10_spmd, body=%wide.region_1.9_spmd.sunk | while | flops 71171840 | bytes 3196933 | solution.py:71
  64.8 10.2 %conditional.4 = ((f32[]{:T(128)}, f32[]{:T(128)}, f32[]{:T(128)}, f32[]{:T(128)}, f32[7,256,256]{1,2,0:T(8,128)S(1)}, /*index=5*/f32[7,256,256]{1,2,0:T(8,128)})) conditional(s32[]{:T(128)} %bitcast.84, (f32[]{:T(128)}, f32[]{:T(128)}, f32[]{:T(128)}, f32[]{:T(128)}, f32[7,256,256]{1,2,0:T(8,128)S(1)}, ...), branch_computations={%region_2.0_spmd, %region_3.8_spmd} | conditional | flops 71171840 | bytes 3196614 | solution.py:67
  69.3 2.6 %multiply_reduce_fusion.2 = (f32[]{:T(128)}, f32[]{:T(128)}, f32[]{:T(128)}, f32[256,256]{0,1:T(8,128)S(1)}) fusion(f32[256,256]{0,1:T(8,128)S(1)} %copy.14, f32[]{:T(128)} %bitcast.4, bf16[256,512]{1,0:T(8,128)(2,1)S(1)} %get-tuple-element.439, bf16[8,256,512]{2,1,0:T(8,128)(2,1)} %get-tuple-element.436, s32[]{:T(128)} %bitcast, ...), kind=kOutput, calls=%fused_computation.13 | convolution fusion | flops 67829760 | bytes 1051660 | tf_op jit(solution)/shard_map/while/body/eval_jaxpr/cond/branch_1_fun/id,jd->ij/dot_general | solution.py:15
  76.2 10.2 %conditional.4 = ((f32[]{:T(128)}, f32[]{:T(128)}, f32[]{:T(128)}, f32[]{:T(128)}, f32[7,256,256]{1,2,0:T(8,128)S(1)}, /*index=5*/f32[7,256,256]{1,2,0:T(8,128)})) conditional(s32[]{:T(128)} %bitcast.84, (f32[]{:T(128)}, f32[]{:T(128)}, f32[]{:T(128)}, f32[]{:T(128)}, f32[7,256,256]{1,2,0:T(8,128)S(1)}, ...), branch_computations={%region_2.0_spmd, %region_3.8_spmd} | conditional | flops 71171840 | bytes 3196614 | solution.py:67
  80.7 2.5 %multiply_reduce_fusion.2 = (f32[]{:T(128)}, f32[]{:T(128)}, f32[]{:T(128)}, f32[256,256]{0,1:T(8,128)S(1)}) fusion(f32[256,256]{0,1:T(8,128)S(1)} %copy.14, f32[]{:T(128)} %bitcast.4, bf16[256,512]{1,0:T(8,128)(2,1)S(1)} %get-tuple-element.439, bf16[8,256,512]{2,1,0:T(8,128)(2,1)} %get-tuple-element.436, s32[]{:T(128)} %bitcast, ...), kind=kOutput, calls=%fused_computation.13 | convolution fusion | flops 67829760 | bytes 1051660 | tf_op jit(solution)/shard_map/while/body/eval_jaxpr/cond/branch_1_fun/id,jd->ij/dot_general | solution.py:15
  87.6 10.2 %conditional.4 = ((f32[]{:T(128)}, f32[]{:T(128)}, f32[]{:T(128)}, f32[]{:T(128)}, f32[7,256,256]{1,2,0:T(8,128)S(1)}, /*index=5*/f32[7,256,256]{1,2,0:T(8,128)})) conditional(s32[]{:T(128)} %bitcast.84, (f32[]{:T(128)}, f32[]{:T(128)}, f32[]{:T(128)}, f32[]{:T(128)}, f32[7,256,256]{1,2,0:T(8,128)S(1)}, ...), branch_computations={%region_2.0_spmd, %region_3.8_spmd} | conditional | flops 71171840 | bytes 3196614 | solution.py:67
  92.1 2.5 %multiply_reduce_fusion.2 = (f32[]{:T(128)}, f32[]{:T(128)}, f32[]{:T(128)}, f32[256,256]{0,1:T(8,128)S(1)}) fusion(f32[256,256]{0,1:T(8,128)S(1)} %copy.14, f32[]{:T(128)} %bitcast.4, bf16[256,512]{1,0:T(8,128)(2,1)S(1)} %get-tuple-element.439, bf16[8,256,512]{2,1,0:T(8,128)(2,1)} %get-tuple-element.436, s32[]{:T(128)} %bitcast, ...), kind=kOutput, calls=%fused_computation.13 | convolution fusion | flops 67829760 | bytes 1051660 | tf_op jit(solution)/shard_map/while/body/eval_jaxpr/cond/branch_1_fun/id,jd->ij/dot_general | solution.py:15
  99.1 10.2 %conditional.4 = ((f32[]{:T(128)}, f32[]{:T(128)}, f32[]{:T(128)}, f32[]{:T(128)}, f32[7,256,256]{1,2,0:T(8,128)S(1)}, /*index=5*/f32[7,256,256]{1,2,0:T(8,128)})) conditional(s32[]{:T(128)} %bitcast.84, (f32[]{:T(128)}, f32[]{:T(128)}, f32[]{:T(128)}, f32[]{:T(128)}, f32[7,256,256]{1,2,0:T(8,128)S(1)}, ...), branch_computations={%region_2.0_spmd, %region_3.8_spmd} | conditional | flops 71171840 | bytes 3196614 | solution.py:67
  103.6 2.5 %multiply_reduce_fusion.2 = (f32[]{:T(128)}, f32[]{:T(128)}, f32[]{:T(128)}, f32[256,256]{0,1:T(8,128)S(1)}) fusion(f32[256,256]{0,1:T(8,128)S(1)} %copy.14, f32[]{:T(128)} %bitcast.4, bf16[256,512]{1,0:T(8,128)(2,1)S(1)} %get-tuple-element.439, bf16[8,256,512]{2,1,0:T(8,128)(2,1)} %get-tuple-element.436, s32[]{:T(128)} %bitcast, ...), kind=kOutput, calls=%fused_computation.13 | convolution fusion | flops 67829760 | bytes 1051660 | tf_op jit(solution)/shard_map/while/body/eval_jaxpr/cond/branch_1_fun/id,jd->ij/dot_general | solution.py:15
  110.5 10.2 %conditional.4 = ((f32[]{:T(128)}, f32[]{:T(128)}, f32[]{:T(128)}, f32[]{:T(128)}, f32[7,256,256]{1,2,0:T(8,128)S(1)}, /*index=5*/f32[7,256,256]{1,2,0:T(8,128)})) conditional(s32[]{:T(128)} %bitcast.84, (f32[]{:T(128)}, f32[]{:T(128)}, f32[]{:T(128)}, f32[]{:T(128)}, f32[7,256,256]{1,2,0:T(8,128)S(1)}, ...), branch_computations={%region_2.0_spmd, %region_3.8_spmd} | conditional | flops 71171840 | bytes 3196614 | solution.py:67
  115.0 2.5 %multiply_reduce_fusion.2 = (f32[]{:T(128)}, f32[]{:T(128)}, f32[]{:T(128)}, f32[256,256]{0,1:T(8,128)S(1)}) fusion(f32[256,256]{0,1:T(8,128)S(1)} %copy.14, f32[]{:T(128)} %bitcast.4, bf16[256,512]{1,0:T(8,128)(2,1)S(1)} %get-tuple-element.439, bf16[8,256,512]{2,1,0:T(8,128)(2,1)} %get-tuple-element.436, s32[]{:T(128)} %bitcast, ...), kind=kOutput, calls=%fused_computation.13 | convolution fusion | flops 67829760 | bytes 1051660 | tf_op jit(solution)/shard_map/while/body/eval_jaxpr/cond/branch_1_fun/id,jd->ij/dot_general | solution.py:15
  122.0 10.2 %conditional.4 = ((f32[]{:T(128)}, f32[]{:T(128)}, f32[]{:T(128)}, f32[]{:T(128)}, f32[7,256,256]{1,2,0:T(8,128)S(1)}, /*index=5*/f32[7,256,256]{1,2,0:T(8,128)})) conditional(s32[]{:T(128)} %bitcast.84, (f32[]{:T(128)}, f32[]{:T(128)}, f32[]{:T(128)}, f32[]{:T(128)}, f32[7,256,256]{1,2,0:T(8,128)S(1)}, ...), branch_computations={%region_2.0_spmd, %region_3.8_spmd} | conditional | flops 71171840 | bytes 3196614 | solution.py:67
  126.5 2.6 %multiply_reduce_fusion.2 = (f32[]{:T(128)}, f32[]{:T(128)}, f32[]{:T(128)}, f32[256,256]{0,1:T(8,128)S(1)}) fusion(f32[256,256]{0,1:T(8,128)S(1)} %copy.14, f32[]{:T(128)} %bitcast.4, bf16[256,512]{1,0:T(8,128)(2,1)S(1)} %get-tuple-element.439, bf16[8,256,512]{2,1,0:T(8,128)(2,1)} %get-tuple-element.436, s32[]{:T(128)} %bitcast, ...), kind=kOutput, calls=%fused_computation.13 | convolution fusion | flops 67829760 | bytes 1051660 | tf_op jit(solution)/shard_map/while/body/eval_jaxpr/cond/branch_1_fun/id,jd->ij/dot_general | solution.py:15
  133.4 10.2 %conditional.4 = ((f32[]{:T(128)}, f32[]{:T(128)}, f32[]{:T(128)}, f32[]{:T(128)}, f32[7,256,256]{1,2,0:T(8,128)S(1)}, /*index=5*/f32[7,256,256]{1,2,0:T(8,128)})) conditional(s32[]{:T(128)} %bitcast.84, (f32[]{:T(128)}, f32[]{:T(128)}, f32[]{:T(128)}, f32[]{:T(128)}, f32[7,256,256]{1,2,0:T(8,128)S(1)}, ...), branch_computations={%region_2.0_spmd, %region_3.8_spmd} | conditional | flops 71171840 | bytes 3196614 | solution.py:67
  137.9 2.5 %multiply_reduce_fusion.2 = (f32[]{:T(128)}, f32[]{:T(128)}, f32[]{:T(128)}, f32[256,256]{0,1:T(8,128)S(1)}) fusion(f32[256,256]{0,1:T(8,128)S(1)} %copy.14, f32[]{:T(128)} %bitcast.4, bf16[256,512]{1,0:T(8,128)(2,1)S(1)} %get-tuple-element.439, bf16[8,256,512]{2,1,0:T(8,128)(2,1)} %get-tuple-element.436, s32[]{:T(128)} %bitcast, ...), kind=kOutput, calls=%fused_computation.13 | convolution fusion | flops 67829760 | bytes 1051660 | tf_op jit(solution)/shard_map/while/body/eval_jaxpr/cond/branch_1_fun/id,jd->ij/dot_general | solution.py:15
  143.6 20.0 %all-reduce = (f32[]{:T(128)}, f32[]{:T(128)}, f32[]{:T(128)}, f32[]{:T(128)}) all-reduce(f32[]{:T(128)} %get-tuple-element.499, f32[]{:T(128)} %get-tuple-element.500, f32[]{:T(128)} %get-tuple-element.502, f32[]{:T(128)} %get-tuple-element.503), channel_id=1, replica_groups=mesh['wide'=8,'narrow'=4] {'wide'}, use_global_device_ids=true, to_apply=%region_10.11 | all-reduce | flops 4 | bytes 32 | tf_op jit(solution)/shard_map/psum | solution.py:9
  163.7 6.3 %all-reduce.1 = (f32[]{:T(128)}, f32[]{:T(128)}, f32[]{:T(128)}, f32[]{:T(128)}) all-reduce(f32[]{:T(128)} %get-tuple-element.585, f32[]{:T(128)} %get-tuple-element.586, f32[]{:T(128)} %get-tuple-element.587, f32[]{:T(128)} %get-tuple-element.588), channel_id=1, replica_groups=mesh['wide'=8,'narrow'=4] {'narrow'}, use_global_device_ids=true, to_apply=%region_11.12 | all-reduce | flops 4 | bytes 32 | tf_op jit(solution)/shard_map/psum | solution.py:9
  173.9 2.7 %copy.17 = f32[7,256,256]{2,1,0:T(8,128)} copy(f32[7,256,256]{1,2,0:T(8,128)} %get-tuple-element.527) | data formatting | bytes 3670016 | tf_op jit(solution)/shard_map/while | solution.py:107
  178.5 59.2 %while.40 = (s32[]{:T(128)}, f32[256,512]{1,0:T(8,128)S(1)}, s32[7]{0:T(128)S(1)}, f32[7,256,256]{2,1,0:T(8,128)}, f32[7,256,256]{2,1,0:T(8,128)S(1)}, /*index=5...) while((s32[]{:T(128)}, f32[256,512]{1,0:T(8,128)S(1)}, ...), condition=%wide.region_20.21_spmd, body=%wide.region_14.20_spmd.sunk | while | flops 139329280 | bytes 5297989 | solution.py:107
  179.8 7.2 %conditional.5 = (f32[256,512]{1,0:T(8,128)S(1)}) conditional(s32[]{:T(128)} %bitcast.85, f32[256,512]{1,0:T(8,128)S(1)} %get-tuple-element.818, (s32[]{:T(128)}, f32[7,256,256]{2,1,0:T(8,128)}, f32[7,256,256]{2,1,0:T(8,128)S(1)}, f32[]{:T(128)}, s32[7]{0:T(128)S(1)}, /*index=5*/s32[8,15,256]{2,1,0:T(8,128)S(1)}, f32[7]{0:T(128)S(1)}, ...), branch_computations={%region_15.15_spmd, %region_16.19_spmd} | conditional | flops 139329280 | bytes 5297766 | solution.py:105
  188.2 7.2 %conditional.5 = (f32[256,512]{1,0:T(8,128)S(1)}) conditional(s32[]{:T(128)} %bitcast.85, f32[256,512]{1,0:T(8,128)S(1)} %get-tuple-element.818, (s32[]{:T(128)}, f32[7,256,256]{2,1,0:T(8,128)}, f32[7,256,256]{2,1,0:T(8,128)S(1)}, f32[]{:T(128)}, s32[7]{0:T(128)S(1)}, /*index=5*/s32[8,15,256]{2,1,0:T(8,128)S(1)}, f32[7]{0:T(128)S(1)}, ...), branch_computations={%region_15.15_spmd, %region_16.19_spmd} | conditional | flops 139329280 | bytes 5297766 | solution.py:105
  193.6 1.8 fusion.10
  196.7 7.2 %conditional.5 = (f32[256,512]{1,0:T(8,128)S(1)}) conditional(s32[]{:T(128)} %bitcast.85, f32[256,512]{1,0:T(8,128)S(1)} %get-tuple-element.818, (s32[]{:T(128)}, f32[7,256,256]{2,1,0:T(8,128)}, f32[7,256,256]{2,1,0:T(8,128)S(1)}, f32[]{:T(128)}, s32[7]{0:T(128)S(1)}, /*index=5*/s32[8,15,256]{2,1,0:T(8,128)S(1)}, f32[7]{0:T(128)S(1)}, ...), branch_computations={%region_15.15_spmd, %region_16.19_spmd} | conditional | flops 139329280 | bytes 5297766 | solution.py:105
  202.0 1.8 fusion.10
  205.1 7.2 %conditional.5 = (f32[256,512]{1,0:T(8,128)S(1)}) conditional(s32[]{:T(128)} %bitcast.85, f32[256,512]{1,0:T(8,128)S(1)} %get-tuple-element.818, (s32[]{:T(128)}, f32[7,256,256]{2,1,0:T(8,128)}, f32[7,256,256]{2,1,0:T(8,128)S(1)}, f32[]{:T(128)}, s32[7]{0:T(128)S(1)}, /*index=5*/s32[8,15,256]{2,1,0:T(8,128)S(1)}, f32[7]{0:T(128)S(1)}, ...), branch_computations={%region_15.15_spmd, %region_16.19_spmd} | conditional | flops 139329280 | bytes 5297766 | solution.py:105
  213.6 7.2 %conditional.5 = (f32[256,512]{1,0:T(8,128)S(1)}) conditional(s32[]{:T(128)} %bitcast.85, f32[256,512]{1,0:T(8,128)S(1)} %get-tuple-element.818, (s32[]{:T(128)}, f32[7,256,256]{2,1,0:T(8,128)}, f32[7,256,256]{2,1,0:T(8,128)S(1)}, f32[]{:T(128)}, s32[7]{0:T(128)S(1)}, /*index=5*/s32[8,15,256]{2,1,0:T(8,128)S(1)}, f32[7]{0:T(128)S(1)}, ...), branch_computations={%region_15.15_spmd, %region_16.19_spmd} | conditional | flops 139329280 | bytes 5297766 | solution.py:105
  219.0 1.8 fusion.10
  222.1 7.2 %conditional.5 = (f32[256,512]{1,0:T(8,128)S(1)}) conditional(s32[]{:T(128)} %bitcast.85, f32[256,512]{1,0:T(8,128)S(1)} %get-tuple-element.818, (s32[]{:T(128)}, f32[7,256,256]{2,1,0:T(8,128)}, f32[7,256,256]{2,1,0:T(8,128)S(1)}, f32[]{:T(128)}, s32[7]{0:T(128)S(1)}, /*index=5*/s32[8,15,256]{2,1,0:T(8,128)S(1)}, f32[7]{0:T(128)S(1)}, ...), branch_computations={%region_15.15_spmd, %region_16.19_spmd} | conditional | flops 139329280 | bytes 5297766 | solution.py:105
  230.5 7.2 %conditional.5 = (f32[256,512]{1,0:T(8,128)S(1)}) conditional(s32[]{:T(128)} %bitcast.85, f32[256,512]{1,0:T(8,128)S(1)} %get-tuple-element.818, (s32[]{:T(128)}, f32[7,256,256]{2,1,0:T(8,128)}, f32[7,256,256]{2,1,0:T(8,128)S(1)}, f32[]{:T(128)}, s32[7]{0:T(128)S(1)}, /*index=5*/s32[8,15,256]{2,1,0:T(8,128)S(1)}, f32[7]{0:T(128)S(1)}, ...), branch_computations={%region_15.15_spmd, %region_16.19_spmd} | conditional | flops 139329280 | bytes 5297766 | solution.py:105
  235.9 1.8 fusion.10
  (137 shorter events, 91.4 us)
Async XLA Ops:
  7.2 10.9 %copy-start.2 = (bf16[256,512]{1,0:T(8,128)(2,1)S(1)}, bf16[256,512]{1,0:T(8,128)(2,1)}, u32[]{:S(2)}) copy-start(bf16[256,512]{1,0:T(8,128)(2,1)} %param.12) | copy-start | bytes 786436
  7.2 11.0 %copy-start.4 = (s32[1,7]{1,0:T(1,128)S(1)}, s32[1,7]{1,0:T(1,128)}, u32[]{:S(2)}) copy-start(s32[1,7]{1,0:T(1,128)} %param.14) | copy-start | bytes 88
  7.2 54.8 %all-gather.2.cloned.1.call-start = ((), (), s32[]{:S(2)}) async-start(), calls=%async_computation.1 | async-start | bytes 2359296 | tf_op jit(solution)/shard_map/all_gather | solution.py:34
  9.8 168.6 %all-to-all-start = ((s32[8,15,256]{2,1,0:T(8,128)}), s32[8,15,256]{2,1,0:T(8,128)S(1)}, u32[]{:S(2)}, u32[]{:S(2)}) async-start(s32[8,15,256]{2,1,0:T(8,128)} %copy.16), calls=%async_computation | async-start | bytes 262144 | tf_op jit(solution)/shard_map/all_to_all | solution.py:85
  62.0 1.6 copy-start.3
  143.6 33.0 %copy-start.1 = (f32[7,256,256]{1,2,0:T(8,128)}, f32[7,256,256]{1,2,0:T(8,128)S(1)}, u32[]{:S(2)}) copy-start(f32[7,256,256]{1,2,0:T(8,128)S(1)} %get-tuple-element.528) | copy-start | bytes 5505028
  237.7 0.8 copy-start
Sparse Core Ops, SparseCore 0:
  10.1 51.8 all-gather.1
